TPU v7x, 128 devices: a whole 4x4x4 slice. The times are simulated.
128 devices in a mesh: wide: 16 (over x, z_lo, core), narrow: 8 (over z_hi, y).
Axes of the slice: x: 4, y: 4, z: 4 (z_hi: 2, z_lo: 2; z = z_hi * 2 + z_lo), core: 2. Of those that a mesh axis runs over, the one named last changes fastest.
Arguments:
- amplitudes: float32 [2, 16, 8, 16, 256, 256], P(None, 'wide', 'narrow'), may hold values from -6 to 6
- low_gate: float32 [2, 256, 256], replicated, may hold values from -0.25 to 0.25
- mid_gate: float32 [2, 256, 256], replicated, may hold values from -0.25 to 0.25
- pair_gates: float32 [3, 2, 4, 4], replicated, may hold values from -2 to 2
Outputs:
- remapped: float32 [2, 16, 8, 16, 256, 256], P(None, 'wide', 'narrow')
All inputs are finite; a program needn't handle non-finite values.
Results may differ from a plain program's by a relative error of at most 0.00007.
Values sent between devices are 32-bit elements; how exact they have to be, the bound alone decides.
No kernel may reach another device: no remote copies, remote signals or barrier semaphores. Data moves between devices by JAX's collectives and lax.ppermute only.
A program may use at most 128 MiB of HBM per device.

v0:
```python
import jax
import jax.numpy as jnp
from jax import lax
from jax.sharding import PartitionSpec as P

highest = lax.Precision.HIGHEST


def swapped(x, axis, bit):
    return lax.ppermute(x, axis, [(i, i ^ 1 << bit) for i in range(lax.axis_size(axis))])


def apply_merged(amplitudes, low_gate, mid_gate):
    real_part, imag_part = (amplitudes[0], amplitudes[1])
    low_real, low_imag = (low_gate[0], low_gate[1])
    first_real = jnp.einsum("abhml,il->abhmi", real_part, low_real, precision=highest) - jnp.einsum(
        "abhml,il->abhmi", imag_part, low_imag, precision=highest
    )
    first_imag = jnp.einsum("abhml,il->abhmi", real_part, low_imag, precision=highest) + jnp.einsum(
        "abhml,il->abhmi", imag_part, low_real, precision=highest
    )
    mid_real, mid_imag = (mid_gate[0], mid_gate[1])
    second_real = jnp.einsum(
        "abhml,im->abhil", first_real, mid_real, precision=highest
    ) - jnp.einsum("abhml,im->abhil", first_imag, mid_imag, precision=highest)
    second_imag = jnp.einsum(
        "abhml,im->abhil", first_real, mid_imag, precision=highest
    ) + jnp.einsum("abhml,im->abhil", first_imag, mid_real, precision=highest)
    return jnp.stack([second_real, second_imag])


def partner_gate(state, other, gate, mine, half_bit):
    rows = lax.dynamic_slice_in_dim(gate, 2 * mine, 2, 1)
    own_cols = lax.dynamic_slice_in_dim(rows, 2 * mine, 2, 2)
    far_cols = lax.dynamic_slice_in_dim(rows, 2 - 2 * mine, 2, 2)
    shape = state.shape
    split_shape = shape[:3] + (shape[3] >> half_bit + 1, 2, 1 << half_bit) + shape[4:]
    own_split = state.reshape(split_shape)
    far_split = other.reshape(split_shape)
    outputs = []
    for target in range(2):
        total_real = jnp.zeros(own_split[0, :, :, :, 0].shape, jnp.float32)
        total_imag = jnp.zeros(own_split[0, :, :, :, 0].shape, jnp.float32)
        for source in range(2):
            for coeffs, piece in ((own_cols, own_split), (far_cols, far_split)):
                amplitude = piece[:, :, :, :, source]
                coef_real = coeffs[0, target, source]
                coef_imag = coeffs[1, target, source]
                total_real = total_real + coef_real * amplitude[0] - coef_imag * amplitude[1]
                total_imag = total_imag + coef_real * amplitude[1] + coef_imag * amplitude[0]
        outputs.append(jnp.stack([total_real, total_imag]))
    return jnp.stack(outputs, axis=4).reshape(shape)


def narrow_gate(state, gate):
    other = swapped(state, "narrow", 1)
    mine = lax.axis_index("narrow") >> 1 & 1
    return partner_gate(state, other, gate, mine, 0)


def remap_qubits(state):
    return lax.all_to_all(state, "wide", split_axis=4, concat_axis=4, tiled=True)


def body(amplitudes, low_gate, mid_gate, pair_gates):
    state = apply_merged(amplitudes, low_gate, mid_gate)
    wide_index = lax.axis_index("wide")
    other = swapped(state, "wide", 0)
    state = partner_gate(state, other, pair_gates[0], wide_index & 1, 0)
    other = swapped(state, "wide", 2)
    state = partner_gate(state, other, pair_gates[1], wide_index >> 2 & 1, 1)
    state = narrow_gate(state, pair_gates[2])
    state = remap_qubits(state)
    return state


def solution(mesh):
    in_specs = (P(None, "wide", "narrow", None, None, None), P(), P(), P())
    out_specs = P(None, "wide", "narrow", None, None, None)
    return jax.shard_map(body, mesh=mesh, in_specs=in_specs, out_specs=out_specs, check_vma=False)
```

profile of v0, /device:TPU:1, one launch (start us, length us, event | category | flops | bytes accessed | tf_op | source)
XLA Modules:
  0.0 675.4 jit_solution(6235137157490432231)
XLA Ops:
  0.0 5.5 fusion.2
  5.5 4.5 fusion
  13.5 6.9 %fusion.42 = f32[16,256,256]{2,1,0:T(8,128)S(1)} fusion(f32[16,256,256]{2,1,0:T(8,128)S(1)} %fusion.12, f32[2,256,256]{2,1,0:T(8,128)S(1)} %copy-done.11), kind=kOutput, calls=%fused_computation.77 | convolution fusion | flops 3221225472 | bytes 8650752 | tf_op jit(solution)/shard_map/abhml,im->abhil/dot_general | solution.py:26
  20.4 7.0 %fusion.46 = f32[16,256,256]{2,1,0:T(8,128)S(1)} fusion(f32[16,256,256]{2,1,0:T(8,128)S(1)} %fusion.12, f32[2,256,256]{2,1,0:T(8,128)S(1)} %copy-done.11), kind=kOutput, calls=%fused_computation.81 | convolution fusion | flops 3221225472 | bytes 8650752 | tf_op jit(solution)/shard_map/abhml,im->abhil/dot_general | solution.py:23
  31.2 7.1 %convolution_add_fusion = f32[16,256,256]{2,1,0:T(8,128)S(1)} fusion(f32[16,256,256]{2,1,0:T(8,128)S(1)} %fusion.42, f32[16,256,256]{2,1,0:T(8,128)S(1)} %fusion.15, f32[2,256,256]{2,1,0:T(8,128)S(1)} %copy-done.11), kind=kOutput, calls=%fused_computation.25 | convolution fusion | flops 3222274048 | bytes 12845056 | tf_op jit(solution)/shard_map/abhml,im->abhil/dot_general | solution.py:28
  38.3 7.2 %convolution_subtract_fusion = f32[16,256,256]{2,1,0:T(8,128)S(1)} fusion(f32[16,256,256]{2,1,0:T(8,128)S(1)} %fusion.46, f32[16,256,256]{2,1,0:T(8,128)S(1)} %fusion.15, f32[2,256,256]{2,1,0:T(8,128)S(1)} %copy-done.11), kind=kOutput, calls=%fused_computation.26 | convolution fusion | flops 3222274048 | bytes 12845056 | tf_op jit(solution)/shard_map/abhml,im->abhil/dot_general | solution.py:25
  51.5 4.6 fusion.62
  58.0 4.6 fusion.63
  72.7 6.9 %fusion.61 = (f32[1,1,1,8,1,1,256,256]{6,7,4,3,0,5,2,1:T(8,128)}, f32[1,1,1,8,1,1,256,256]{6,7,4,3,0,5,2,1:T(8,128)}, f32[1,1,1,8,1,1,256,256]{6,7,4,3,0,5,2,1:T(8,128)}, f32[1,1,1,8,1,1,256,256]{6,7,4,3,0,5,2,1:T(8,128)}) fusion(f32[2,1,1,8,2,1,256,256]{6,7,4,3,0,5,2,1:T(8,128)} %bitcast.33), kind=kLoop, calls=%fused_computation.102 | loop fusion | bytes 16777216 | tf_op jit(solution)/shard_map/slice | solution.py:49
  91.2 11.9 %add_subtract_fusion = (f32[1,1,1,8,1,1,256,256]{7,6,3,5,4,2,1,0:T(8,128)S(1)}, f32[1,1,1,8,1,1,256,256]{7,6,3,5,4,2,1,0:T(8,128)S(1)}) fusion(f32[1,1,1,8,1,1,256,256]{7,6,3,5,4,2,1,0:T(8,128)} %copy.188, f32[1,1,1,8,1,1,256,256]{7,6,3,5,4,2,1,0:T(8,128)} %copy.187, f32[1,1,1,8,1,1,256,256]{7,6,3,5,4,2,1,0:T(8,128)S(1)} %copy.186, ...), kind=kLoop, calls=%fused_computation.74 | loop fusion | flops 15728640 | bytes 20971552 | tf_op jit(solution)/shard_map/sub | solution.py:49
  106.6 6.9 %add_subtract_fusion.1 = (f32[1,1,1,8,1,1,256,256]{7,6,3,5,4,2,1,0:T(8,128)S(1)}, f32[1,1,1,8,1,1,256,256]{7,6,3,5,4,2,1,0:T(8,128)S(1)}) fusion(f32[1,1,1,8,1,1,256,256]{7,6,3,5,4,2,1,0:T(8,128)S(1)} %copy-done.6, f32[1,1,1,8,1,1,256,256]{7,6,3,5,4,2,1,0:T(8,128)S(1)} %copy-done.7, f32[1,1,1,8,1,1,256,256]{7,6,3,5,4,2,1,0:T(8,128)S(1)} %copy.186, ...), kind=kLoop, calls=%fused_computation.76 | loop fusion | flops 15728640 | bytes 20971552 | tf_op jit(solution)/shard_map/sub | solution.py:49
  128.1 172.1 %collective-permute-done.1 = f32[2,1,1,16,256,256]{5,4,3,0,2,1:T(8,128)S(1)} collective-permute-done((f32[2,1,1,16,256,256]{5,4,3,0,2,1:T(8,128)}, f32[2,1,1,16,256,256]{5,4,3,0,2,1:T(8,128)S(1)}, u32[]{:S(2)}, u32[]{:S(2)}) %collective-permute-start.1) | collective-permute-done | bytes 8388640 | tf_op jit(solution)/shard_map/ppermute | solution.py:10
  300.2 6.0 fusion.33
  306.2 6.0 fusion.41
  312.2 6.1 fusion.39
  318.2 6.1 fusion.36
  333.5 179.3 %collective-permute-done.2 = f32[2,1,1,16,256,256]{5,4,3,0,2,1:T(8,128)} collective-permute-done((f32[2,1,1,16,256,256]{5,4,3,0,2,1:T(8,128)}, f32[2,1,1,16,256,256]{5,4,3,0,2,1:T(8,128)}, u32[]{:S(2)}, u32[]{:S(2)}) %collective-permute-start.2) | collective-permute-done | bytes 8388640 | tf_op jit(solution)/shard_map/ppermute | solution.py:10
  512.8 11.5 %fusion.18 = f32[1,1,1,8,1,256,256]{6,5,3,4,2,1,0:T(8,128)S(1)} fusion(f32[2,1,1,8,2,1,256,256]{7,6,4,3,0,5,2,1:T(8,128)} %bitcast.92, f32[2,1,1,8,2,1,256,256]{7,6,4,3,0,5,2,1:T(8,128)} %bitcast.97, f32[]{:T(128)} %bitcast.117, f32[]{:T(128)} %bitcast.116, f32[]{:T(128)} %bitcast.114, f32[]{:T(128)} %bitcast.113, f32[]{:T(128)} %bitcast.112, f32[]{:T(128)} %bitcast.111, ...), kind=kLoop, calls=%fused_computation.38 | loop fusion | flops 7864320 | bytes 18874400 | tf_op jit(solution)/shard_map/add | solution.py:50
  524.4 11.3 %fusion.32 = f32[1,1,1,8,1,256,256]{6,5,3,4,2,1,0:T(8,128)S(1)} fusion(f32[2,1,1,8,2,1,256,256]{7,6,4,3,0,5,2,1:T(8,128)} %bitcast.92, f32[2,1,1,8,2,1,256,256]{7,6,4,3,0,5,2,1:T(8,128)} %bitcast.97, f32[]{:T(128)} %bitcast.117, f32[]{:T(128)} %bitcast.116, f32[]{:T(128)} %bitcast.114, f32[]{:T(128)} %bitcast.113, f32[]{:T(128)} %bitcast.112, f32[]{:T(128)} %bitcast.111, ...), kind=kLoop, calls=%fused_computation.58 | loop fusion | flops 7864320 | bytes 18874400 | tf_op jit(solution)/shard_map/sub | solution.py:49
  535.7 11.3 %fusion.28 = f32[1,1,1,8,1,256,256]{6,5,3,0,4,2,1:T(8,128)S(1)} fusion(f32[2,1,1,8,2,1,256,256]{7,6,4,3,0,5,2,1:T(8,128)} %bitcast.92, f32[2,1,1,8,2,1,256,256]{7,6,4,3,0,5,2,1:T(8,128)} %bitcast.97, f32[]{:T(128)} %bitcast.103, f32[]{:T(128)} %bitcast.102, f32[]{:T(128)} %bitcast.100, f32[]{:T(128)} %bitcast.99, f32[]{:T(128)} %bitcast.98, f32[]{:T(128)} %bitcast.95, ...), kind=kLoop, calls=%fused_computation.54 | loop fusion | flops 7864320 | bytes 18874400 | tf_op jit(solution)/shard_map/add | solution.py:50
  547.0 11.3 %fusion.23 = f32[1,1,1,8,1,256,256]{6,5,3,0,4,2,1:T(8,128)S(1)} fusion(f32[2,1,1,8,2,1,256,256]{7,6,4,3,0,5,2,1:T(8,128)} %bitcast.92, f32[2,1,1,8,2,1,256,256]{7,6,4,3,0,5,2,1:T(8,128)} %bitcast.97, f32[]{:T(128)} %bitcast.103, f32[]{:T(128)} %bitcast.102, f32[]{:T(128)} %bitcast.100, f32[]{:T(128)} %bitcast.99, f32[]{:T(128)} %bitcast.98, f32[]{:T(128)} %bitcast.95, ...), kind=kLoop, calls=%fused_computation.49 | loop fusion | flops 7864320 | bytes 18874400 | tf_op jit(solution)/shard_map/sub | solution.py:49
  560.6 4.9 copy.172
  565.5 101.3 %all_to_all.5 = f32[2,1,1,16,256,256]{5,3,0,2,1,4:T(8,128)S(1)} all-to-all(f32[2,1,1,16,256,256]{5,3,0,2,1,4:T(8,128)S(1)} %copy.172), channel_id=1, replica_groups=mesh['wide'=16,'narrow'=8] {'wide'}, dimensions={4} | all-to-all | bytes 16777216 | tf_op jit(solution)/shard_map/all_to_all | solution.py:62
  666.8 8.3 %copy.173 = f32[2,1,1,16,256,256]{5,4,3,2,1,0:T(8,128)} copy(f32[2,1,1,16,256,256]{5,3,0,2,1,4:T(8,128)S(1)} %all_to_all.5) | data formatting | bytes 16777216 | tf_op jit(solution)/shard_map/all_to_all | solution.py:62
  (62 shorter events, 66.4 us)
Async XLA Ops:
  0.0 5.5 copy-start.2
  5.5 4.5 copy-start.10
  10.0 3.5 copy-start.11
  38.3 7.3 %copy-start.1 = (f32[16,256,256]{2,1,0:T(8,128)}, f32[16,256,256]{2,1,0:T(8,128)S(1)}, u32[]{:S(2)}) copy-start(f32[16,256,256]{2,1,0:T(8,128)S(1)} %convolution_add_fusion) | copy-start | bytes 12582916
  45.5 4.5 copy-start
  50.0 22.7 %collective-permute-start = (f32[2,1,1,16,256,256]{4,5,3,2,1,0:T(8,128)}, f32[2,1,1,16,256,256]{4,5,3,2,1,0:T(8,128)}, u32[]{:S(2)}, u32[]{:S(2)}) collective-permute-start(f32[2,1,1,16,256,256]{4,5,3,2,1,0:T(8,128)} %pad_maximum_fusion), channel_id=1, source_target_pairs={{0,8},{8,0},{16,24},{24,16},{32,40},{40,32},{48,56},{56,48},{64,72... | collective-permute-start | bytes 25165832 | tf_op jit(solution)/shard_map/ppermute | solution.py:10
  68.4 2.9 copy-start.12
  91.2 12.4 %copy-start.7 = (f32[1,1,1,8,1,1,256,256]{7,6,3,5,4,2,1,0:T(8,128)S(1)}, f32[1,1,1,8,1,1,256,256]{7,6,3,5,4,2,1,0:T(8,128)}, u32[]{:S(2)}) copy-start(f32[1,1,1,8,1,1,256,256]{7,6,3,5,4,2,1,0:T(8,128)} %copy.187) | copy-start | bytes 6291460
  91.2 12.4 %copy-start.8 = (f32[1,1,1,8,1,1,256,256]{7,6,3,5,4,2,1,0:T(8,128)S(1)}, f32[1,1,1,8,1,1,256,256]{7,6,3,5,4,2,1,0:T(8,128)}, u32[]{:S(2)}) copy-start(f32[1,1,1,8,1,1,256,256]{7,6,3,5,4,2,1,0:T(8,128)} %copy.184) | copy-start | bytes 6291460
  91.2 12.4 %copy-start.9 = (f32[1,1,1,8,1,1,256,256]{7,6,3,5,4,2,1,0:T(8,128)S(1)}, f32[1,1,1,8,1,1,256,256]{7,6,3,5,4,2,1,0:T(8,128)}, u32[]{:S(2)}) copy-start(f32[1,1,1,8,1,1,256,256]{7,6,3,5,4,2,1,0:T(8,128)} %copy.183) | copy-start | bytes 6291460
  103.1 1.6 copy-start.3
  103.1 2.2 copy-start.4
  103.2 2.8 copy-start.5
  103.2 3.4 copy-start.6
  117.9 182.3 %collective-permute-start.1 = (f32[2,1,1,16,256,256]{5,4,3,0,2,1:T(8,128)}, f32[2,1,1,16,256,256]{5,4,3,0,2,1:T(8,128)S(1)}, u32[]{:S(2)}, u32[]{:S(2)}) collective-permute-start(f32[2,1,1,16,256,256]{5,4,3,0,2,1:T(8,128)} %bitcast.372), channel_id=1, source_target_pairs={{0,32},{8,40},{16,48},{24,56},{32,0},{40,8},{48,16},{56,24},{64,96... | collective-permute-start | bytes 25165832 | tf_op jit(solution)/shard_map/ppermute | solution.py:10
  329.7 183.1 %collective-permute-start.2 = (f32[2,1,1,16,256,256]{5,4,3,0,2,1:T(8,128)}, f32[2,1,1,16,256,256]{5,4,3,0,2,1:T(8,128)}, u32[]{:S(2)}, u32[]{:S(2)}) collective-permute-start(f32[2,1,1,16,256,256]{5,4,3,0,2,1:T(8,128)} %bitcast.96), channel_id=1, source_target_pairs={{0,2},{1,3},{2,0},{3,1},{4,6},{5,7},{6,4},{7,5},{8,10},{9,11},{10,... | collective-permute-start | bytes 25165832 | tf_op jit(solution)/shard_map/ppermute | solution.py:10
where the time goes:
time: 686 us; the launch traced here: 675 us
  waiting for transfers between devices  351 us (51%)
  other arithmetic  104 us (15%)
  blocking collectives  101 us (15%)
  local copies, waits for them, and re-layouts  66.9 us (10%)
  matrix products  45.4 us (7%)
    ppermute x3, waiting for transfers between devices, swapped(): lax.ppermute(x, axis, [(i, i ^ 1 << bit) for i in range(lax.axis_size(axi...  351 us
    all_to_all x1, blocking collectives, remap_qubits(): lax.all_to_all(state, 'wide', split_axis=4, concat_axis=4, tiled=True)  101 us
    sub x6, other arithmetic, partner_gate(): total_real + coef_real * amplitude[0] - coef_imag * amplitude[1]  53.5 us
    add x4, other arithmetic, partner_gate(): total_imag + coef_real * amplitude[1] + coef_imag * amplitude[0]  34.9 us
    unnamed x34, local copies, waits for them, and re-layouts  25.4 us
  transfers between devices with their start and end apart: 3, of which 2 were waited for; matrix products, arithmetic and copies ran while one was open for 5% of the time, Pallas kernels for 0%

commit v1 on v0

--- a/solution.py
+++ b/solution.py
@@ -59,7 +59,10 @@
 
 
 def remap_qubits(state):
-    return lax.all_to_all(state, "wide", split_axis=4, concat_axis=4, tiled=True)
+    return jnp.concatenate(
+        lax.all_to_all(jnp.stack(jnp.split(state, lax.axis_size("wide"), axis=4)), "wide", 0, 0),
+        axis=4,
+    )
 
 
 def body(amplitudes, low_gate, mid_gate, pair_gates):

time: 686 us -> 667 us (0.972)
  local copies, waits for them, and re-layouts: 66.9 us -> 17.6 us
  other arithmetic: 104 us -> 126 us
  waiting for transfers between devices: 351 us -> 362 us
    unnamed x34 -> x31, local copies, waits for them, and re-layouts: 25.4 us -> 0.79 us
    add x4 -> x6, other arithmetic: 34.9 us -> 53.1 us  [partner_gate(): total_imag + coef_real * amplitude[1] + coef_imag * amplitude[0]]
    slice x2 -> x0, local copies, waits for them, and re-layouts: 11.5 us -> none  [partner_gate(): amplitude[1]]
    ppermute x3, waiting for transfers between devices: 351 us -> 362 us  [swapped(): lax.ppermute(x, axis, [(i, i ^ 1 << bit) for i in range(lax.axis_size(axi...]
    all_to_all x1 -> x0, local copies, waits for them, and re-layouts: 8.25 us -> none  [remap_qubits(): lax.all_to_all(state, 'wide', split_axis=4, concat_axis=4, tiled=True)]
  transfers between devices with their start and end apart: 3 -> 3, of which waited for: 2 -> 3; matrix products, arithmetic and copies ran while one was open for 5% -> 2% of each run, Pallas kernels for 0% -> 0%
where the time goes in v1:
time: 667 us; the launch traced here: 656 us
  waiting for transfers between devices  362 us (54%)
  other arithmetic  126 us (19%)
  blocking collectives  101 us (15%)
  matrix products  43.1 us (6%)
  local copies, waits for them, and re-layouts  17.6 us (3%)
    ppermute x3, waiting for transfers between devices, swapped(): lax.ppermute(x, axis, [(i, i ^ 1 << bit) for i in range(lax.axis_size(axi...  362 us
    all_to_all x1, blocking collectives, remap_qubits(): lax.all_to_all(jnp.stack(jnp.split(state, lax.axis_size('wide'), axis=4))...  101 us
    sub x6, other arithmetic, partner_gate(): total_real + coef_real * amplitude[0] - coef_imag * amplitude[1]  56.6 us
    add x6, other arithmetic, partner_gate(): total_imag + coef_real * amplitude[1] + coef_imag * amplitude[0]  53.1 us
  transfers between devices with their start and end apart: 3, of which 3 were waited for; matrix products, arithmetic and copies ran while one was open for 2% of the time, Pallas kernels for 0%

profile of v1, /device:TPU:1, one launch (start us, length us, event | category | flops | bytes accessed | tf_op | source)
XLA Modules:
  0.0 656.3 jit_solution(12506741555727102593)
XLA Ops:
  0.0 5.5 fusion.2
  5.5 4.5 fusion
  13.5 4.3 fusion.62
  17.8 12.8 %fusion.58 = f32[16,256,256]{1,2,0:T(8,128)S(1)} fusion(f32[16,256,256]{2,1,0:T(8,128)S(1)} %fusion.12, f32[2,256,256]{2,1,0:T(8,128)S(1)} %copy-done.6), kind=kOutput, calls=%fused_computation.117 | convolution fusion | flops 3221225472 | bytes 8650752 | tf_op jit(solution)/shard_map/abhml,im->abhil/dot_general | solution.py:26
  34.2 4.4 convolution_subtract_fusion
  38.6 4.6 convolution_add_fusion
  43.3 4.3 pad_maximum_fusion
  50.6 11.7 %collective-permute-done = f32[2,1,1,16,256,256]{5,4,3,2,1,0:T(8,128)} collective-permute-done((f32[2,1,1,16,256,256]{5,4,3,2,1,0:T(8,128)}, f32[2,1,1,16,256,256]{5,4,3,2,1,0:T(8,128)}, u32[]{:S(2)}, u32[]{:S(2)}) %collective-permute-start) | collective-permute-done | bytes 8388640 | tf_op jit(solution)/shard_map/ppermute | solution.py:10
  62.3 12.6 %add_subtract_fusion.1 = f32[1,1,1,8,1,1,256,256]{7,6,3,5,4,2,1,0:T(8,128)S(1)} fusion(f32[1,1,1,8,2,1,256,256]{7,6,4,3,5,2,1,0:T(8,128)} %bitcast.504, f32[1,1,1,8,2,1,256,256]{7,6,4,3,5,2,1,0:T(8,128)} %bitcast.509, f32[2,1,1,8,2,1,256,256]{7,6,4,3,0,5,2,1:T(8,128)} %bitcast.33, f32[]{:T(128)} %bitcast.40, f32[]{:T(128)} %bitcast.39, f32[]{:T(128)} %bitcast.37, ...), kind=kLoop, calls=%fused_computation.84 | loop fusion | flops 7864320 | bytes 18874400 | tf_op jit(solution)/shard_map/sub | solution.py:49
  74.9 9.1 %add_add_fusion.1 = f32[1,1,1,8,1,1,256,256]{7,6,3,5,4,2,1,0:T(8,128)S(1)} fusion(f32[1,1,1,8,2,1,256,256]{7,6,4,3,5,2,1,0:T(8,128)S(1)} %bitcast.505, f32[1,1,1,8,2,1,256,256]{7,6,4,3,5,2,1,0:T(8,128)S(1)} %bitcast.510, f32[2,1,1,8,2,1,256,256]{7,6,4,3,0,5,2,1:T(8,128)} %bitcast.33, f32[]{:T(128)} %bitcast.40, f32[]{:T(128)} %bitcast.39, f32[]{:T(128)} %bitcast.37, ...), kind=kLoop, calls=%fused_computation.83 | loop fusion | flops 7864320 | bytes 18874400 | tf_op jit(solution)/shard_map/add | solution.py:50
  84.0 9.0 %add_subtract_fusion = f32[1,1,1,8,1,1,256,256]{7,6,3,5,4,2,1,0:T(8,128)S(1)} fusion(f32[1,1,1,8,2,1,256,256]{7,6,4,3,5,2,1,0:T(8,128)S(1)} %bitcast.506, f32[1,1,1,8,2,1,256,256]{7,6,4,3,5,2,1,0:T(8,128)S(1)} %bitcast.511, f32[2,1,1,8,2,1,256,256]{7,6,4,3,0,5,2,1:T(8,128)} %bitcast.33, f32[]{:T(128)} %bitcast.50, f32[]{:T(128)} %bitcast.49, f32[]{:T(128)} %bitcast.48, ...), kind=kLoop, calls=%fused_computation.82 | loop fusion | flops 7864320 | bytes 18874400 | tf_op jit(solution)/shard_map/sub | solution.py:49
  93.0 9.0 %add_add_fusion = f32[1,1,1,8,1,1,256,256]{7,6,3,5,4,2,1,0:T(8,128)S(1)} fusion(f32[1,1,1,8,2,1,256,256]{7,6,4,3,5,2,1,0:T(8,128)S(1)} %bitcast.507, f32[1,1,1,8,2,1,256,256]{7,6,4,3,5,2,1,0:T(8,128)S(1)} %bitcast.512, f32[2,1,1,8,2,1,256,256]{7,6,4,3,0,5,2,1:T(8,128)} %bitcast.33, f32[]{:T(128)} %bitcast.50, f32[]{:T(128)} %bitcast.49, f32[]{:T(128)} %bitcast.48, ...), kind=kLoop, calls=%fused_computation.81 | loop fusion | flops 7864320 | bytes 18874400 | tf_op jit(solution)/shard_map/add | solution.py:50
  117.3 171.4 %collective-permute-done.1 = f32[2,1,1,16,256,256]{5,4,3,0,2,1:T(8,128)S(1)} collective-permute-done((f32[2,1,1,16,256,256]{5,4,3,0,2,1:T(8,128)}, f32[2,1,1,16,256,256]{5,4,3,0,2,1:T(8,128)S(1)}, u32[]{:S(2)}, u32[]{:S(2)}) %collective-permute-start.1) | collective-permute-done | bytes 8388640 | tf_op jit(solution)/shard_map/ppermute | solution.py:10
  288.6 6.1 fusion.36
  294.8 6.1 fusion.39
  300.9 6.1 fusion.41
  307.0 6.1 fusion.33
  322.3 178.9 %collective-permute-done.2 = f32[2,1,1,16,256,256]{5,4,3,0,2,1:T(8,128)} collective-permute-done((f32[2,1,1,16,256,256]{5,4,3,0,2,1:T(8,128)}, f32[2,1,1,16,256,256]{5,4,3,0,2,1:T(8,128)}, u32[]{:S(2)}, u32[]{:S(2)}) %collective-permute-start.2) | collective-permute-done | bytes 8388640 | tf_op jit(solution)/shard_map/ppermute | solution.py:10
  501.2 11.4 %fusion.23 = f32[1,1,1,8,1,256,256]{6,5,3,0,4,2,1:T(8,128)S(1)} fusion(f32[2,1,1,8,2,1,256,256]{7,6,4,3,0,5,2,1:T(8,128)} %bitcast.92, f32[2,1,1,8,2,1,256,256]{7,6,4,3,0,5,2,1:T(8,128)} %bitcast.97, f32[]{:T(128)} %bitcast.103, f32[]{:T(128)} %bitcast.102, f32[]{:T(128)} %bitcast.100, f32[]{:T(128)} %bitcast.99, f32[]{:T(128)} %bitcast.98, f32[]{:T(128)} %bitcast.95, ...), kind=kLoop, calls=%fused_computation.57 | loop fusion | flops 7864320 | bytes 18874400 | tf_op jit(solution)/shard_map/sub | solution.py:49
  512.6 11.4 %fusion.28 = f32[1,1,1,8,1,256,256]{6,5,3,0,4,2,1:T(8,128)S(1)} fusion(f32[2,1,1,8,2,1,256,256]{7,6,4,3,0,5,2,1:T(8,128)} %bitcast.92, f32[2,1,1,8,2,1,256,256]{7,6,4,3,0,5,2,1:T(8,128)} %bitcast.97, f32[]{:T(128)} %bitcast.103, f32[]{:T(128)} %bitcast.102, f32[]{:T(128)} %bitcast.100, f32[]{:T(128)} %bitcast.99, f32[]{:T(128)} %bitcast.98, f32[]{:T(128)} %bitcast.95, ...), kind=kLoop, calls=%fused_computation.62 | loop fusion | flops 7864320 | bytes 18874400 | tf_op jit(solution)/shard_map/add | solution.py:50
  524.0 11.4 %fusion.32 = f32[1,1,1,8,1,256,256]{6,5,3,4,2,1,0:T(8,128)S(1)} fusion(f32[2,1,1,8,2,1,256,256]{7,6,4,3,0,5,2,1:T(8,128)} %bitcast.92, f32[2,1,1,8,2,1,256,256]{7,6,4,3,0,5,2,1:T(8,128)} %bitcast.97, f32[]{:T(128)} %bitcast.117, f32[]{:T(128)} %bitcast.116, f32[]{:T(128)} %bitcast.114, f32[]{:T(128)} %bitcast.113, f32[]{:T(128)} %bitcast.112, f32[]{:T(128)} %bitcast.111, ...), kind=kLoop, calls=%fused_computation.66 | loop fusion | flops 7864320 | bytes 18874400 | tf_op jit(solution)/shard_map/sub | solution.py:49
  535.4 11.4 %fusion.18 = f32[1,1,1,8,1,256,256]{6,5,3,4,2,1,0:T(8,128)S(1)} fusion(f32[2,1,1,8,2,1,256,256]{7,6,4,3,0,5,2,1:T(8,128)} %bitcast.92, f32[2,1,1,8,2,1,256,256]{7,6,4,3,0,5,2,1:T(8,128)} %bitcast.97, f32[]{:T(128)} %bitcast.117, f32[]{:T(128)} %bitcast.116, f32[]{:T(128)} %bitcast.114, f32[]{:T(128)} %bitcast.113, f32[]{:T(128)} %bitcast.112, f32[]{:T(128)} %bitcast.111, ...), kind=kLoop, calls=%fused_computation.46 | loop fusion | flops 7864320 | bytes 18874400 | tf_op jit(solution)/shard_map/add | solution.py:50
  549.9 101.5 %all_to_all.5 = f32[16,2,1,1,16,16,256]{6,5,4,1,3,2,0:T(8,128)S(1)} all-to-all(f32[16,2,1,1,16,16,256]{6,5,4,1,3,2,0:T(8,128)S(1)} %fusion.42), channel_id=1, replica_groups=mesh['wide'=16,'narrow'=8] {'wide'}, dimensions={0} | all-to-all | bytes 16777216 | tf_op jit(solution)/shard_map/all_to_all | solution.py:63
  651.4 4.4 copy.191
  (58 shorter events, 37.4 us)
Async XLA Ops:
  0.0 5.5 copy-start.4
  5.5 4.5 copy-start.5
  10.0 3.5 copy-start.6
  38.6 4.6 copy-start
  43.2 4.5 copy-start.2
  43.3 5.9 copy-start.7
  47.7 14.5 %collective-permute-start = (f32[2,1,1,16,256,256]{5,4,3,2,1,0:T(8,128)}, f32[2,1,1,16,256,256]{5,4,3,2,1,0:T(8,128)}, u32[]{:S(2)}, u32[]{:S(2)}) collective-permute-start(f32[2,1,1,16,256,256]{5,4,3,2,1,0:T(8,128)} %pad_maximum_fusion), channel_id=1, source_target_pairs={{0,8},{8,0},{16,24},{24,16},{32,40},{40,32},{48,56},{56,48},{64,72... | collective-permute-start | bytes 25165832 | tf_op jit(solution)/shard_map/ppermute | solution.py:10
  62.3 12.6 %copy-start.1 = (f32[16,256,256]{1,2,0:T(8,128)S(1)}, f32[16,256,256]{1,2,0:T(8,128)}, u32[]{:S(2)}) copy-start(f32[16,256,256]{1,2,0:T(8,128)} %copy-done) | copy-start | bytes 12582916
  62.3 12.6 %copy-start.3 = (f32[16,256,256]{1,2,0:T(8,128)S(1)}, f32[16,256,256]{1,2,0:T(8,128)}, u32[]{:S(2)}) copy-start(f32[16,256,256]{1,2,0:T(8,128)} %copy-done.2) | copy-start | bytes 12582916
  106.8 181.9 %collective-permute-start.1 = (f32[2,1,1,16,256,256]{5,4,3,0,2,1:T(8,128)}, f32[2,1,1,16,256,256]{5,4,3,0,2,1:T(8,128)S(1)}, u32[]{:S(2)}, u32[]{:S(2)}) collective-permute-start(f32[2,1,1,16,256,256]{5,4,3,0,2,1:T(8,128)} %bitcast.542), channel_id=1, source_target_pairs={{0,32},{8,40},{16,48},{24,56},{32,0},{40,8},{48,16},{56,24},{64,96... | collective-permute-start | bytes 25165832 | tf_op jit(solution)/shard_map/ppermute | solution.py:10
  318.6 182.6 %collective-permute-start.2 = (f32[2,1,1,16,256,256]{5,4,3,0,2,1:T(8,128)}, f32[2,1,1,16,256,256]{5,4,3,0,2,1:T(8,128)}, u32[]{:S(2)}, u32[]{:S(2)}) collective-permute-start(f32[2,1,1,16,256,256]{5,4,3,0,2,1:T(8,128)} %bitcast.96), channel_id=1, source_target_pairs={{0,2},{1,3},{2,0},{3,1},{4,6},{5,7},{6,4},{7,5},{8,10},{9,11},{10,... | collective-permute-start | bytes 25165832 | tf_op jit(solution)/shard_map/ppermute | solution.py:10
